TPU v7x, 768 devices: a whole 4x8x12 slice. The times are simulated.
768 devices in a mesh: dp: 8 (over y), tensor: 96 (over z, x, core).
Axes of the slice: x: 4, y: 8, z: 12, core: 2. Of those that a mesh axis runs over, the one named last changes fastest.
Arguments:
- grad_out: bfloat16 [1536, 8192], P('dp'), may hold values from -6 to 6
- gate_act: bfloat16 [1536, 16896], P('dp', 'tensor'), may hold values from -20 to 20
- up_act: bfloat16 [1536, 16896], P('dp', 'tensor'), may hold values from -6 to 6
- w_gate: bfloat16 [16896, 8192], P('tensor'), may hold values from -0.0625 to 0.0625
- w_up: bfloat16 [16896, 8192], P('tensor'), may hold values from -0.0625 to 0.0625
- w_down: bfloat16 [16896, 8192], P('tensor'), may hold values from -0.046875 to 0.046875
Outputs:
- input_grad: bfloat16 [1536, 8192], P(('dp', 'tensor'))
- down_grad: bfloat16 [16896, 8192], P('tensor', 'dp')
All inputs are finite; a program needn't handle non-finite values.
Results may differ from a plain program's by a relative error of at most 0.014.
Values may be sent and summed in bfloat16 or wider, within the bound.
No kernel may reach another device: no remote copies, remote signals or barrier semaphores. Data moves between devices by JAX's collectives and lax.ppermute only.
A program may use at most 64 MiB of HBM per device.

v0:
```python
import jax
import jax.numpy as jnp
import numpy as np
from jax import lax
from jax.experimental import pallas as pl
from jax.experimental.pallas import tpu as pltpu
from jax.sharding import Mesh, PartitionSpec as P

NY, NZ, NX, NC = 8, 12, 4, 2
PLANE = ("z", "x", "c")
CHUNKS = 4
PIECES = 4
LANES = 128
f32, bf16 = jnp.float32, jnp.bfloat16


VMEM = pl.BlockSpec(memory_space=pltpu.VMEM)
HBM = pl.BlockSpec(memory_space=pltpu.HBM)


def shift(n, d):
    return [(i, (i + d) % n) for i in range(n)]


def round_x(step):
    return [
        (x * NC + c, (x + step * (1 - 2 * c)) % NX * NC + c)
        for x in range(NX)
        for c in range(NC)
    ]


def dot(a, b, over):
    return lax.dot_general(a, b, (over, ((), ())), preferred_element_type=f32)


def one_hot(order):
    n = order.shape[0]
    cols = lax.broadcasted_iota(jnp.int32, (n, n), 1)
    return jnp.where(cols == order, 1.0, 0.0).astype(bf16)


def tables(tokens):
    share = tokens // (NX * NC)
    per = share // NZ
    i = np.arange(tokens)
    j, k, rest = i // (NX * share), (i // share) % NX, i % share
    by_owner = (rest // per) * (NX * NC * per) + rest % per
    return np.stack([k, j, rest, by_owner], axis=1).astype(np.int32)


def rows_of(table, base, x_step, c_step):
    c = (lax.axis_index("c") + table[:, 1:2]) & (NC - 1)
    x = (lax.axis_index("x") + table[:, 0:1] * (1 - 2 * c)) & (NX - 1)
    return table[:, base : base + 1] + x * x_step + c * c_step


def pack_kernel(
    table_hbm, gate_hbm, up_hbm, grad_hbm, packed_hbm,
    table, gate_v, up_v, grad, mine, hid, small_sem, grad_sem, mine_sem, hid_sem,
):
    ff, tokens = gate_v.shape
    ny, mine_rows, width = mine.shape
    share = grad.shape[1]
    small = [
        pltpu.make_async_copy(a, b, small_sem.at[i])
        for i, (a, b) in enumerate(
            ((gate_hbm, gate_v), (up_hbm, up_v), (table_hbm, table))
        )
    ]
    x, c = lax.axis_index("x"), lax.axis_index("c")
    for n in range(2):
        first = (((x + 2 * n) & (NX - 1)) * NC + c) * share
        rows = pl.ds(pl.multiple_of(first, 8), share)
        small.append(
            pltpu.make_async_copy(grad_hbm.at[rows, :], grad.at[n], grad_sem.at[n])
        )
    for copy in small:
        copy.start()
    for copy in small[:3]:
        copy.wait()
    gate = gate_v[...].astype(f32)
    hidden = (gate * jax.nn.sigmoid(gate) * up_v[...].astype(f32)).astype(bf16)
    order = rows_of(table[...], 2, NC * share, share)
    hidden = dot(one_hot(order), hidden, ((1,), (1,))).astype(bf16)
    half, quarter = tokens // 2, tokens // 4
    for n in range(2):
        lanes = slice(n * LANES, (n + 1) * LANES)
        hid[:half, lanes] = hidden[n * half : (n + 1) * half, :LANES]
    rest = jnp.zeros((quarter, LANES // 2 - (ff - LANES)), bf16)
    for n in range(2):
        lanes = slice(n * LANES, (n + 1) * LANES)
        groups = []
        for m in (2 * n, 2 * n + 1):
            groups += [hidden[m * quarter : (m + 1) * quarter, LANES:], rest]
        hid[half:, lanes] = jnp.concatenate(groups, axis=1)
    stores = [
        pltpu.make_async_copy(hid, packed_hbm.at[y, mine_rows:, :], hid_sem.at[y])
        for y in range(ny)
    ]
    for copy in stores:
        copy.start()
    for copy in small[3:]:
        copy.wait()
    for y in range(ny):
        for n in range(2):
            for b in range(PIECES):
                start = (y * PIECES + b) * width
                row = (n * PIECES + b) * share
                mine[y, row : row + share, :] = grad[n, :, start : start + width]
        copy = pltpu.make_async_copy(
            mine.at[y], packed_hbm.at[y, :mine_rows, :], mine_sem.at[y]
        )
        copy.start()
        stores.append(copy)
    for copy in stores:
        copy.wait()


def main_kernel(
    table_hbm, gate_hbm, up_hbm, grad_hbm, wd_hbm, wg_hbm, wu_hbm,
    their_far, their_near, our_far, our_near,
    table, gate_v, up_v, grad, wd, w, small_sem, grad_sem, wd_sem, wg_sem, wu_sem,
):
    _, d = grad.shape
    ff = wd.shape[0]
    blk = our_far.shape[0]
    step = d // CHUNKS
    chunks = [pl.ds(i * step, step) for i in range(CHUNKS)]
    small = [
        pltpu.make_async_copy(a, b, small_sem.at[i])
        for i, (a, b) in enumerate(
            ((gate_hbm, gate_v), (up_hbm, up_v), (table_hbm, table))
        )
    ]
    loads = [
        (
            pltpu.make_async_copy(grad_hbm.at[:, c], grad.at[:, c], grad_sem.at[i]),
            pltpu.make_async_copy(wd_hbm.at[:, c], wd.at[:, c], wd_sem.at[i]),
        )
        for i, c in enumerate(chunks)
    ]
    weights = [
        (
            pltpu.make_async_copy(wg_hbm.at[:, c], w.at[:ff, c], wg_sem.at[i]),
            pltpu.make_async_copy(wu_hbm.at[:, c], w.at[ff:, c], wu_sem.at[i]),
        )
        for i, c in enumerate(chunks)
    ]
    for copy in small:
        copy.start()
    for pair in loads + weights:
        for copy in pair:
            copy.start()

    for copy in small:
        copy.wait()
    gate = gate_v[...].astype(f32)
    up = up_v[...].astype(f32)
    sig = jax.nn.sigmoid(gate)
    silu = gate * sig
    slope = up * sig * (1.0 + gate * (1.0 - sig))
    per = blk // NZ
    pick = one_hot(rows_of(table[...], 3, NC * per, per))
    hidden_grad = jnp.zeros(gate.shape, f32)
    for pair, c in zip(loads, chunks):
        for copy in pair:
            copy.wait()
        hidden_grad = hidden_grad + dot(wd[:, c], grad[:, c], ((1,), (1,)))
    both = jnp.concatenate(
        [(hidden_grad * slope).astype(bf16), (hidden_grad * silu).astype(bf16)], axis=0
    )
    both = dot(pick, both, ((1,), (1,))).astype(bf16)
    for i, pair in enumerate(weights):
        for copy in pair:
            copy.wait()
        for n in range(step // 512):
            at = slice(i * step + n * 512, i * step + (n + 1) * 512)
            part = dot(both, w[:, at], ((1,), (0,))).astype(bf16)
            for far, near, first in (
                (our_far, our_near, 0),
                (their_far, their_near, NX),
            ):
                rows = [
                    part[(first + k) * blk : (first + k + 1) * blk] for k in range(NX)
                ]
                near[:blk, at] = rows[0]
                near[blk : 2 * blk, at] = rows[1]
                far[:, at] = rows[2]
                near[2 * blk :, at] = rows[3]


def add_kernel(a_ref, b_ref, out_ref):
    out_ref[...] = (a_ref[...].astype(f32) + b_ref[...].astype(f32)).astype(bf16)


def near_kernel(a_ref, b_ref, own_ref, via_ref, other_ref):
    blk = own_ref.shape[0]
    for n, ref in enumerate((own_ref, via_ref, other_ref)):
        rows = slice(n * blk, (n + 1) * blk)
        total = a_ref[rows].astype(f32) + b_ref[rows].astype(f32)
        ref[...] = total.astype(ref.dtype)


def own_kernel(own_ref, via_ref, other_ref, out_ref):
    nz, per, _ = out_ref.shape
    total = own_ref[...] + via_ref[...].astype(f32) + other_ref[...].astype(f32)
    for z in range(nz):
        out_ref[z] = total[z * per : (z + 1) * per].astype(bf16)


def total_kernel(parts_ref, out_ref):
    total = parts_ref[0].astype(f32)
    for z in range(1, parts_ref.shape[0]):
        total = total + parts_ref[z].astype(f32)
    out_ref[...] = total.astype(bf16)


def gather_rows(jks, piece_of, own_ref, h, g):
    ny, _, width = own_ref.shape
    block = h.shape[0] // len(jks)
    share = block // ny
    for n, jk in enumerate(jks):
        rows = slice(n * block, (n + 1) * block)
        first = 2 * PIECES * share
        at, lane = first + jk % 4 * share, jk // 4 * LANES
        h[rows, :LANES] = own_ref[:, at : at + share, lane : lane + LANES].reshape(
            block, LANES
        )
        at, lane = first + (4 + jk % 2) * share, jk // 2 * (LANES // 2)
        h[rows, LANES:] = own_ref[
            :, at : at + share, lane : lane + h.shape[1] - LANES
        ].reshape(block, h.shape[1] - LANES)
        for b in range(PIECES):
            piece = piece_of(jk, b, share)
            g[rows, b * width : (b + 1) * width] = piece.reshape(block, width)


def down_kernel(own_ref, side_ref, core_ref, out_ref, h, g):
    def piece_of(jk, b, share):
        first = (jk % NX // 2 * PIECES + b) * share
        ref = side_ref if jk % 2 else (own_ref if jk < NX else core_ref)
        return ref[:, first : first + share, :]

    gather_rows((0, 1, 2, 3, NX, NX + 2), piece_of, own_ref, h, g)
    left = h[...]
    width = own_ref.shape[2]
    for b in range(PIECES):
        c = slice(b * width, (b + 1) * width)
        out_ref[:, c] = dot(left, g[:, c], ((0,), (0,)))


def last_kernel(own_ref, side_ref, sum_ref, out_ref, h, g):
    def piece_of(jk, b, share):
        first = (jk % NX // 2 * PIECES + b) * share
        return side_ref[:, first : first + share, :]

    gather_rows((NX + 1, NX + 3), piece_of, own_ref, h, g)
    left = h[...]
    width = own_ref.shape[2]
    for b in range(PIECES):
        c = slice(b * width, (b + 1) * width)
        part = dot(left, g[:, c], ((0,), (0,)))
        out_ref[:, c] = (sum_ref[:, c] + part).astype(bf16)


def call(kernel, specs, outs, flops, nbytes, scratch=(), in_hbm=(), auto=False, mib=16, dtype=None):
    dtypes = dtype or (bf16,) * len(outs)
    run = pl.pallas_call(
        kernel,
        in_specs=specs,
        out_specs=[HBM if n in in_hbm else VMEM for n in range(len(outs))],
        out_shape=[
            jax.ShapeDtypeStruct(s, t) if auto or n in in_hbm else pltpu.VMEM(s, t)
            for n, (s, t) in enumerate(zip(outs, dtypes))
        ],
        scratch_shapes=list(scratch),
        compiler_params=pltpu.CompilerParams(vmem_limit_bytes=mib << 20),
        cost_estimate=pl.CostEstimate(
            flops=flops, bytes_accessed=nbytes, transcendentals=0
        ),
    )

    def on_chip(*args):
        made = run(
            *(
                pltpu.with_memory_space_constraint(a, pltpu.VMEM) if s is VMEM else a
                for a, s in zip(args, specs)
            )
        )
        return [
            o if auto or n in in_hbm else pltpu.with_memory_space_constraint(o, pltpu.VMEM)
            for n, o in enumerate(made)
        ]

    return on_chip


def local(grad_out, gate_act, up_act, w_gate, w_up, w_down):
    tokens, d = grad_out.shape
    ff = gate_act.shape[1]
    share = tokens // (NX * NC)
    cols = d // NY
    width = cols // PIECES
    blk = tokens // NC // NX
    table = jnp.asarray(tables(tokens))
    gate_t, up_t = gate_act.T, up_act.T

    packed_rows = 2 * PIECES * share + tokens // 2 + tokens // 4
    dma = pltpu.SemaphoreType.DMA
    small = [
        pltpu.VMEM(table.shape, jnp.int32),
        pltpu.VMEM((ff, tokens), bf16),
        pltpu.VMEM((ff, tokens), bf16),
    ]
    (packed,) = call(
        pack_kernel,
        [HBM] * 4,
        [(NY, packed_rows, width)],
        2 * tokens * tokens * ff,
        4_000_000,
        small
        + [
            pltpu.VMEM((2, share, d), bf16),
            pltpu.VMEM((NY, 2 * PIECES * share, width), bf16),
            pltpu.VMEM((packed_rows - 2 * PIECES * share, width), bf16),
            dma((3,)),
            dma((2,)),
            dma((NY,)),
            dma((NY,)),
        ],
        in_hbm=(0,),
        mib=63,
    )(table, gate_t, up_t, grad_out)
    packed = lax.all_to_all(packed, "y", 0, 0)

    their_far, their_near, our_far, our_near = call(
        main_kernel,
        [HBM] * 7,
        [(blk, d), (3 * blk, d), (blk, d), (3 * blk, d)],
        6 * tokens * ff * d,
        15_000_000,
        small
        + [
            pltpu.VMEM((tokens, d), bf16),
            pltpu.VMEM((ff, d), bf16),
            pltpu.VMEM((2 * ff, d), bf16),
            dma((3,)),
        ]
        + [dma((CHUNKS,))] * 4,
        mib=58,
    )(table, gate_t, up_t, grad_out, w_down, w_gate, w_up)
    their_far = lax.ppermute(their_far, "c", shift(NC, 1))
    their_near = lax.ppermute(their_near, "c", shift(NC, 1))
    (far,) = call(add_kernel, [VMEM] * 2, [(blk, d)], blk * d, 6 * blk * d)(
        our_far, their_far
    )
    far = lax.ppermute(far, ("x", "c"), round_x(1))
    own, via, other = call(
        near_kernel,
        [VMEM] * 2,
        [(blk, d)] * 3,
        3 * blk * d,
        22 * blk * d,
        dtype=(f32, f32, bf16),
    )(our_near, their_near)
    other = lax.ppermute(other, ("x", "c"), round_x(-1))
    (via,) = call(add_kernel, [VMEM] * 2, [(blk, d)], blk * d, 8 * blk * d)(via, far)
    via = lax.ppermute(via, ("x", "c"), round_x(1))
    (own,) = call(
        own_kernel, [VMEM] * 3, [(NZ, blk // NZ, d)], 2 * blk * d, 10 * blk * d
    )(own, via, other)
    parts = lax.all_to_all(own, "z", 0, 0)
    (input_grad,) = call(
        total_kernel, [VMEM], [(blk // NZ, d)], blk * d, 3 * blk * d, auto=True
    )(parts)

    mine = packed[:, : 2 * PIECES * share, :]
    side = lax.ppermute(mine, ("x", "c"), round_x(-1))
    core = lax.ppermute(mine, "c", shift(NC, 1))
    side_core = lax.ppermute(side, "c", shift(NC, 1))
    early, late = 6 * NY * share, 2 * NY * share
    (part,) = call(
        down_kernel,
        [VMEM] * 3,
        [(ff, cols)],
        2 * early * ff * cols,
        6_000_000,
        [pltpu.VMEM((early, ff), bf16), pltpu.VMEM((early, cols), bf16)],
        dtype=(f32,),
    )(packed, side, core)
    (down_grad,) = call(
        last_kernel,
        [VMEM] * 3,
        [(ff, cols)],
        2 * late * ff * cols,
        3_000_000,
        [pltpu.VMEM((late, ff), bf16), pltpu.VMEM((late, cols), bf16)],
        auto=True,
    )(packed, side_core, part)
    return (input_grad, down_grad)


def solution(mesh):
    mesh4 = Mesh(mesh.devices.reshape(NY, NZ, NX, NC), ("y",) + PLANE)
    placed = (
        P("y", None),
        P("y", PLANE),
        P("y", PLANE),
        P(PLANE, None),
        P(PLANE, None),
        P(PLANE, None),
    )
    return jax.shard_map(
        local,
        mesh=mesh4,
        in_specs=placed,
        out_specs=(P(("y",) + PLANE, None), P(PLANE, "y")),
        check_vma=False,
    )
```

profile of v0, /device:TPU:65, one launch (start us, length us, event | category | flops | bytes accessed | tf_op | source)
XLA Modules:
  0.0 109.5 jit_solution(6860809347503135978)
XLA Ops:
  0.6 2.7 %shard_map.92 = bf16[8,336,256]{2,1,0:T(8,128)(2,1)} custom-call(s32[192,4]{1,0:T(8,128)} %constant.2.clone.table_hbm, bf16[176,192]{1,0:T(8,128)(2,1)} %bitcast.2, bf16[176,192]{1,0:T(8,128)(2,1)} %bitcast.4, bf16[192,8192]{1,0:T(8,128)(2,1)} %grad_hbm.3), custom_call_target="tpu_custom_call" | custom-call | flops 12976128 | bytes 4000000 | tf_op jit(solution)/shard_map/pallas_call | solution.py:285
  3.3 6.8 %all-to-all-start.1 = ((bf16[8,336,256]{2,1,0:T(8,128)(2,1)}), bf16[8,336,256]{2,1,0:T(8,128)(2,1)S(1)}, u32[]{:S(2)}, u32[]{:S(2)}) async-start(bf16[8,336,256]{2,1,0:T(8,128)(2,1)} %shard_map.92), calls=%async_computation.1 | async-start | bytes 2752512 | tf_op jit(solution)/shard_map/all_to_all | solution.py:335
  10.2 10.5 %shard_map.86 = (bf16[24,8192]{1,0:T(8,128)(2,1)S(1)}, bf16[72,8192]{1,0:T(8,128)(2,1)}, bf16[24,8192]{1,0:T(8,128)(2,1)S(1)}, bf16[72,8192]{1,0:T(8,128)(2,1)S(1)}) custom-call(s32[192,4]{1,0:T(8,128)} %constant.2.clone.table_hbm, bf16[176,192]{1,0:T(8,128)(2,1)} %bitcast.3, bf16[176,192]{1,0:T(8,128)(2,1)} %bitcast.5, bf16[192,8192]{1,0:T(8,128)(2,1)} %grad_hbm.3, ...), custom_call_target="tpu_custom_call" | custom-call | flops 1660944384 | bytes 15000000 | tf_op jit(solution)/shard_map/pallas_call | solution.py:285
  20.7 2.9 %collective-permute-start = (bf16[72,8192]{1,0:T(8,128)(2,1)}, bf16[72,8192]{1,0:T(8,128)(2,1)}, u32[]{:S(2)}, u32[]{:S(2)}) collective-permute-start(bf16[72,8192]{1,0:T(8,128)(2,1)} %get-tuple-element.10), channel_id=1, source_target_pairs={{0,1},{1,0},{2,3},{3,2},{4,5},{5,4},{6,7},{7,6},{8,9},{9,8},{10,11... | collective-permute-start | bytes 3538952 | tf_op jit(solution)/shard_map/ppermute | solution.py:354
  23.6 1.9 %collective-permute-start.1 = (bf16[24,8192]{1,0:T(8,128)(2,1)S(1)}, bf16[24,8192]{1,0:T(8,128)(2,1)S(1)}, u32[]{:S(2)}, u32[]{:S(2)}) collective-permute-start(bf16[24,8192]{1,0:T(8,128)(2,1)S(1)} %get-tuple-element.14), channel_id=1, source_target_pairs={{0,1},{1,0},{2,3},{3,2},{4,5},{5,4},{6,7},{7,6},{8,9},{9,8},{10,11... | collective-permute-start | bytes 1179656 | tf_op jit(solution)/shard_map/ppermute | solution.py:353
  25.5 1.7 %collective-permute-done.1.b_ref = bf16[24,8192]{1,0:T(8,128)(2,1)S(1)} collective-permute-done((bf16[24,8192]{1,0:T(8,128)(2,1)S(1)}, bf16[24,8192]{1,0:T(8,128)(2,1)S(1)}, u32[]{:S(2)}, u32[]{:S(2)}) %collective-permute-start.1) | collective-permute-done | bytes 393248 | tf_op jit(solution)/shard_map/ppermute | solution.py:353
  27.2 0.1 shard_map.88
  27.3 4.4 %collective-permute-start.2 = (bf16[24,8192]{1,0:T(8,128)(2,1)S(1)}, bf16[24,8192]{1,0:T(8,128)(2,1)S(1)}, u32[]{:S(2)}, u32[]{:S(2)}) collective-permute-start(bf16[24,8192]{1,0:T(8,128)(2,1)S(1)} %shard_map.88), channel_id=1, source_target_pairs={{0,2},{1,7},{2,4},{3,1},{4,6},{5,3},{6,0},{7,5},{8,10},{9,15},{10,... | collective-permute-start | bytes 1179656 | tf_op jit(solution)/shard_map/ppermute | solution.py:358
  31.7 14.7 %all-to-all-done.1.own_ref = bf16[8,336,256]{2,1,0:T(8,128)(2,1)S(1)} async-done(((bf16[8,336,256]{2,1,0:T(8,128)(2,1)}), bf16[8,336,256]{2,1,0:T(8,128)(2,1)S(1)}, u32[]{:S(2)}, u32[]{:S(2)}) %all-to-all-start.1) | async-done | bytes 1376288 | tf_op jit(solution)/shard_map/all_to_all | solution.py:335
  46.4 0.9 slice.4
  47.3 3.1 %collective-permute-start.5 = (bf16[8,192,256]{2,1,0:T(8,128)(2,1)}, bf16[8,192,256]{2,1,0:T(8,128)(2,1)}, u32[]{:S(2)}, u32[]{:S(2)}) collective-permute-start(bf16[8,192,256]{2,1,0:T(8,128)(2,1)} %slice.4), channel_id=1, source_target_pairs={{0,6},{1,3},{2,0},{3,5},{4,2},{5,7},{6,4},{7,1},{8,14},{9,11},{10,... | collective-permute-start | bytes 2359304 | tf_op jit(solution)/shard_map/ppermute | solution.py:379
  50.5 0.0 collective-permute-done.b_ref
  50.5 1.5 %shard_map.87 = (f32[24,8192]{1,0:T(8,128)S(1)}, f32[24,8192]{1,0:T(8,128)S(1)}, bf16[24,8192]{1,0:T(8,128)(2,1)S(1)}) custom-call(bf16[72,8192]{1,0:T(8,128)(2,1)S(1)} %get-tuple-element.9.a_ref, bf16[72,8192]{1,0:T(8,128)(2,1)} %collective-permute-done.b_ref), custom_call_target="tpu_custom_call" | custom-call | flops 589824 | bytes 4325376 | tf_op jit(solution)/shard_map/pallas_call | solution.py:285
  52.0 0.0 collective-permute-done.2.b_ref
  52.0 0.1 shard_map.89
  52.1 3.4 %collective-permute-start.3 = (bf16[24,8192]{1,0:T(8,128)(2,1)S(1)}, bf16[24,8192]{1,0:T(8,128)(2,1)S(1)}, u32[]{:S(2)}, u32[]{:S(2)}) collective-permute-start(bf16[24,8192]{1,0:T(8,128)(2,1)S(1)} %shard_map.89), channel_id=1, source_target_pairs={{0,2},{1,7},{2,4},{3,1},{4,6},{5,3},{6,0},{7,5},{8,10},{9,15},{10,... | collective-permute-start | bytes 1179656 | tf_op jit(solution)/shard_map/ppermute | solution.py:369
  55.5 1.9 %collective-permute-start.4 = (bf16[24,8192]{1,0:T(8,128)(2,1)S(1)}, bf16[24,8192]{1,0:T(8,128)(2,1)S(1)}, u32[]{:S(2)}, u32[]{:S(2)}) collective-permute-start(bf16[24,8192]{1,0:T(8,128)(2,1)S(1)} %get-tuple-element.15), channel_id=1, source_target_pairs={{0,6},{1,3},{2,0},{3,5},{4,2},{5,7},{6,4},{7,1},{8,14},{9,11},{10,... | collective-permute-start | bytes 1179656 | tf_op jit(solution)/shard_map/ppermute | solution.py:367
  57.4 7.8 %collective-permute-done.3.via_ref = bf16[24,8192]{1,0:T(8,128)(2,1)S(1)} collective-permute-done((bf16[24,8192]{1,0:T(8,128)(2,1)S(1)}, bf16[24,8192]{1,0:T(8,128)(2,1)S(1)}, u32[]{:S(2)}, u32[]{:S(2)}) %collective-permute-start.3) | collective-permute-done | bytes 393248 | tf_op jit(solution)/shard_map/ppermute | solution.py:369
  65.2 4.7 %collective-permute-done.4.other_ref = bf16[24,8192]{1,0:T(8,128)(2,1)S(1)} collective-permute-done((bf16[24,8192]{1,0:T(8,128)(2,1)S(1)}, bf16[24,8192]{1,0:T(8,128)(2,1)S(1)}, u32[]{:S(2)}, u32[]{:S(2)}) %collective-permute-start.4) | collective-permute-done | bytes 393248 | tf_op jit(solution)/shard_map/ppermute | solution.py:367
  69.9 0.9 shard_map.90
  70.8 14.2 %all-to-all-start = ((bf16[12,2,8192]{2,1,0:T(2,128)(2,1)}), bf16[12,2,8192]{2,1,0:T(2,128)(2,1)S(1)}, u32[]{:S(2)}, u32[]{:S(2)}) async-start(bf16[12,2,8192]{2,1,0:T(2,128)(2,1)} %shard_map.90), calls=%async_computation | async-start | bytes 786432 | tf_op jit(solution)/shard_map/all_to_all | solution.py:373
  85.0 3.2 %collective-permute-start.7 = (bf16[8,192,256]{2,1,0:T(8,128)(2,1)}, bf16[8,192,256]{2,1,0:T(8,128)(2,1)S(1)}, u32[]{:S(2)}, u32[]{:S(2)}) collective-permute-start(bf16[8,192,256]{2,1,0:T(8,128)(2,1)} %slice.4), channel_id=1, source_target_pairs={{0,1},{1,0},{2,3},{3,2},{4,5},{5,4},{6,7},{7,6},{8,9},{9,8},{10,11... | collective-permute-start | bytes 2359304 | tf_op jit(solution)/shard_map/ppermute | solution.py:380
  88.2 0.0 collective-permute-done.5.side_ref
  88.2 1.9 %collective-permute-start.6 = (bf16[8,192,256]{2,1,0:T(8,128)(2,1)}, bf16[8,192,256]{2,1,0:T(8,128)(2,1)S(1)}, u32[]{:S(2)}, u32[]{:S(2)}) collective-permute-start(bf16[8,192,256]{2,1,0:T(8,128)(2,1)} %collective-permute-done.5.side_ref), channel_id=1, source_target_pairs={{0,1},{1,0},{2,3},{3,2},{4,5},{5,4},{6,7},{7,6},{8,9},{9,8},{10,11... | collective-permute-start | bytes 2359304 | tf_op jit(solution)/shard_map/ppermute | solution.py:381
  90.2 15.4 %all-to-all-done.parts_ref = bf16[12,2,8192]{2,1,0:T(2,128)(2,1)S(1)} async-done(((bf16[12,2,8192]{2,1,0:T(2,128)(2,1)}), bf16[12,2,8192]{2,1,0:T(2,128)(2,1)S(1)}, u32[]{:S(2)}, u32[]{:S(2)}) %all-to-all-start) | async-done | bytes 393248 | tf_op jit(solution)/shard_map/all_to_all | solution.py:373
  105.6 0.7 shard_map.91
  106.3 0.0 collective-permute-done.7.core_ref
  106.3 2.0 %shard_map.93.sum_ref = f32[176,1024]{1,0:T(8,128)S(1)} custom-call(bf16[8,336,256]{2,1,0:T(8,128)(2,1)S(1)} %all-to-all-done.1.own_ref, bf16[8,192,256]{2,1,0:T(8,128)(2,1)} %collective-permute-done.5.side_ref, bf16[8,192,256]{2,1,0:T(8,128)(2,1)S(1)} %collective-permute-done.7.core_ref), custom_call_target="tpu_custom_call" | custom-call | flops 415236096 | bytes 6000000 | tf_op jit(solution)/shard_map/pallas_call | solution.py:285
  108.3 0.0 collective-permute-done.6.side_ref
  108.3 1.2 %shard_map.94 = bf16[176,1024]{1,0:T(8,128)(2,1)} custom-call(bf16[8,336,256]{2,1,0:T(8,128)(2,1)S(1)} %all-to-all-done.1.own_ref, bf16[8,192,256]{2,1,0:T(8,128)(2,1)S(1)} %collective-permute-done.6.side_ref, f32[176,1024]{1,0:T(8,128)S(1)} %shard_map.93.sum_ref), custom_call_target="tpu_custom_call" | custom-call | flops 138412032 | bytes 3000000 | tf_op jit(solution)/shard_map/pallas_call | solution.py:285
Async XLA Ops:
  3.3 43.0 %all-to-all-start.1 = ((bf16[8,336,256]{2,1,0:T(8,128)(2,1)}), bf16[8,336,256]{2,1,0:T(8,128)(2,1)S(1)}, u32[]{:S(2)}, u32[]{:S(2)}) async-start(bf16[8,336,256]{2,1,0:T(8,128)(2,1)} %shard_map.92), calls=%async_computation.1 | async-start | bytes 2752512 | tf_op jit(solution)/shard_map/all_to_all | solution.py:335
  20.7 29.8 %collective-permute-start = (bf16[72,8192]{1,0:T(8,128)(2,1)}, bf16[72,8192]{1,0:T(8,128)(2,1)}, u32[]{:S(2)}, u32[]{:S(2)}) collective-permute-start(bf16[72,8192]{1,0:T(8,128)(2,1)} %get-tuple-element.10), channel_id=1, source_target_pairs={{0,1},{1,0},{2,3},{3,2},{4,5},{5,4},{6,7},{7,6},{8,9},{9,8},{10,11... | collective-permute-start | bytes 3538952 | tf_op jit(solution)/shard_map/ppermute | solution.py:354
  23.6 3.6 %collective-permute-start.1 = (bf16[24,8192]{1,0:T(8,128)(2,1)S(1)}, bf16[24,8192]{1,0:T(8,128)(2,1)S(1)}, u32[]{:S(2)}, u32[]{:S(2)}) collective-permute-start(bf16[24,8192]{1,0:T(8,128)(2,1)S(1)} %get-tuple-element.14), channel_id=1, source_target_pairs={{0,1},{1,0},{2,3},{3,2},{4,5},{5,4},{6,7},{7,6},{8,9},{9,8},{10,11... | collective-permute-start | bytes 1179656 | tf_op jit(solution)/shard_map/ppermute | solution.py:353
  27.3 24.7 %collective-permute-start.2 = (bf16[24,8192]{1,0:T(8,128)(2,1)S(1)}, bf16[24,8192]{1,0:T(8,128)(2,1)S(1)}, u32[]{:S(2)}, u32[]{:S(2)}) collective-permute-start(bf16[24,8192]{1,0:T(8,128)(2,1)S(1)} %shard_map.88), channel_id=1, source_target_pairs={{0,2},{1,7},{2,4},{3,1},{4,6},{5,3},{6,0},{7,5},{8,10},{9,15},{10,... | collective-permute-start | bytes 1179656 | tf_op jit(solution)/shard_map/ppermute | solution.py:358
  47.3 40.9 %collective-permute-start.5 = (bf16[8,192,256]{2,1,0:T(8,128)(2,1)}, bf16[8,192,256]{2,1,0:T(8,128)(2,1)}, u32[]{:S(2)}, u32[]{:S(2)}) collective-permute-start(bf16[8,192,256]{2,1,0:T(8,128)(2,1)} %slice.4), channel_id=1, source_target_pairs={{0,6},{1,3},{2,0},{3,5},{4,2},{5,7},{6,4},{7,1},{8,14},{9,11},{10,... | collective-permute-start | bytes 2359304 | tf_op jit(solution)/shard_map/ppermute | solution.py:379
  52.1 13.1 %collective-permute-start.3 = (bf16[24,8192]{1,0:T(8,128)(2,1)S(1)}, bf16[24,8192]{1,0:T(8,128)(2,1)S(1)}, u32[]{:S(2)}, u32[]{:S(2)}) collective-permute-start(bf16[24,8192]{1,0:T(8,128)(2,1)S(1)} %shard_map.89), channel_id=1, source_target_pairs={{0,2},{1,7},{2,4},{3,1},{4,6},{5,3},{6,0},{7,5},{8,10},{9,15},{10,... | collective-permute-start | bytes 1179656 | tf_op jit(solution)/shard_map/ppermute | solution.py:369
  55.5 14.5 %collective-permute-start.4 = (bf16[24,8192]{1,0:T(8,128)(2,1)S(1)}, bf16[24,8192]{1,0:T(8,128)(2,1)S(1)}, u32[]{:S(2)}, u32[]{:S(2)}) collective-permute-start(bf16[24,8192]{1,0:T(8,128)(2,1)S(1)} %get-tuple-element.15), channel_id=1, source_target_pairs={{0,6},{1,3},{2,0},{3,5},{4,2},{5,7},{6,4},{7,1},{8,14},{9,11},{10,... | collective-permute-start | bytes 1179656 | tf_op jit(solution)/shard_map/ppermute | solution.py:367
  70.8 34.7 %all-to-all-start = ((bf16[12,2,8192]{2,1,0:T(2,128)(2,1)}), bf16[12,2,8192]{2,1,0:T(2,128)(2,1)S(1)}, u32[]{:S(2)}, u32[]{:S(2)}) async-start(bf16[12,2,8192]{2,1,0:T(2,128)(2,1)} %shard_map.90), calls=%async_computation | async-start | bytes 786432 | tf_op jit(solution)/shard_map/all_to_all | solution.py:373
  85.0 21.2 %collective-permute-start.7 = (bf16[8,192,256]{2,1,0:T(8,128)(2,1)}, bf16[8,192,256]{2,1,0:T(8,128)(2,1)S(1)}, u32[]{:S(2)}, u32[]{:S(2)}) collective-permute-start(bf16[8,192,256]{2,1,0:T(8,128)(2,1)} %slice.4), channel_id=1, source_target_pairs={{0,1},{1,0},{2,3},{3,2},{4,5},{5,4},{6,7},{7,6},{8,9},{9,8},{10,11... | collective-permute-start | bytes 2359304 | tf_op jit(solution)/shard_map/ppermute | solution.py:380
  88.2 20.1 %collective-permute-start.6 = (bf16[8,192,256]{2,1,0:T(8,128)(2,1)}, bf16[8,192,256]{2,1,0:T(8,128)(2,1)S(1)}, u32[]{:S(2)}, u32[]{:S(2)}) collective-permute-start(bf16[8,192,256]{2,1,0:T(8,128)(2,1)} %collective-permute-done.5.side_ref), channel_id=1, source_target_pairs={{0,1},{1,0},{2,3},{3,2},{4,5},{5,4},{6,7},{7,6},{8,9},{9,8},{10,11... | collective-permute-start | bytes 2359304 | tf_op jit(solution)/shard_map/ppermute | solution.py:381
where the time goes:
time: 110 us
  waiting for transfers between devices  44.3 us (40%)
  starting transfers between devices  43.7 us (40%)
  Pallas kernels  19.8 us (18%)
    pallas_call x9, Pallas kernels, on_chip(): run(*(pltpu.with_memory_space_constraint(a, pltpu.VMEM) if s is VMEM else...  19.8 us
    all_to_all x1, waiting for transfers between devices, local(): parts = lax.all_to_all(own, 'z', 0, 0)  15.4 us
    all_to_all x1, waiting for transfers between devices, local(): packed = lax.all_to_all(packed, 'y', 0, 0)  14.7 us
    all_to_all x1, starting transfers between devices, local(): parts = lax.all_to_all(own, 'z', 0, 0)  14.2 us
    ppermute x1, waiting for transfers between devices, local(): via = lax.ppermute(via, ('x', 'c'), round_x(1))  7.82 us
    all_to_all x1, starting transfers between devices, local(): packed = lax.all_to_all(packed, 'y', 0, 0)  6.83 us
    ppermute x1, waiting for transfers between devices, local(): other = lax.ppermute(other, ('x', 'c'), round_x(-1))  4.71 us
    ppermute x1, starting transfers between devices, local(): far = lax.ppermute(far, ('x', 'c'), round_x(1))  4.38 us
  transfers between devices with their start and end apart: 10, of which 5 were waited for; matrix products, arithmetic and copies ran while one was open for 1% of the time, Pallas kernels for 14%

commit v1 on v0

--- a/solution.py
+++ b/solution.py
@@ -9,6 +9,7 @@
 NY, NZ, NX, NC = 8, 12, 4, 2
 PLANE = ("z", "x", "c")
 CHUNKS = 4
+HEAD = 2
 PIECES = 4
 LANES = 128
 f32, bf16 = jnp.float32, jnp.bfloat16
@@ -55,9 +56,39 @@
     return table[:, base : base + 1] + x * x_step + c * c_step
 
 
+def load_chunks(grad_hbm, wd_hbm, grad, wd, grad_sem, wd_sem, first):
+    step = grad_hbm.shape[1] // CHUNKS
+    pairs = []
+    for i in range(grad.shape[1] // step):
+        here, there = pl.ds((first + i) * step, step), pl.ds(i * step, step)
+        pairs.append(
+            (
+                pltpu.make_async_copy(
+                    grad_hbm.at[:, here], grad.at[:, there], grad_sem.at[i]
+                ),
+                pltpu.make_async_copy(wd_hbm.at[:, here], wd.at[:, there], wd_sem.at[i]),
+            )
+        )
+    return pairs
+
+
+def contract(loads, grad, wd, behind=()):
+    step = grad.shape[1] // len(loads)
+    total = jnp.zeros((wd.shape[0], grad.shape[0]), f32)
+    for i, pair in enumerate(loads):
+        for copy in pair:
+            copy.wait()
+        for copy in behind[i * len(behind) // len(loads) :][: len(behind) // len(loads)]:
+            copy.start()
+        at = slice(i * step, (i + 1) * step)
+        total = total + dot(wd[:, at], grad[:, at], ((1,), (1,)))
+    return total
+
+
 def pack_kernel(
-    table_hbm, gate_hbm, up_hbm, grad_hbm, packed_hbm,
-    table, gate_v, up_v, grad, mine, hid, small_sem, grad_sem, mine_sem, hid_sem,
+    table_hbm, gate_hbm, up_hbm, grad_hbm, wd_hbm, packed_hbm, part_ref,
+    table, gate_v, up_v, grad, mine, hid, gradc, wd,
+    small_sem, grad_sem, mine_sem, hid_sem, gradc_sem, wd_sem,
 ):
     ff, tokens = gate_v.shape
     ny, mine_rows, width = mine.shape
@@ -75,8 +106,12 @@
         small.append(
             pltpu.make_async_copy(grad_hbm.at[rows, :], grad.at[n], grad_sem.at[n])
         )
+    loads = load_chunks(grad_hbm, wd_hbm, gradc, wd, gradc_sem, wd_sem, 0)
     for copy in small:
         copy.start()
+    for pair in loads:
+        for copy in pair:
+            copy.start()
     for copy in small[:3]:
         copy.wait()
     gate = gate_v[...].astype(f32)
@@ -113,16 +148,17 @@
         )
         copy.start()
         stores.append(copy)
+    part_ref[...] = contract(loads, gradc, wd)
     for copy in stores:
         copy.wait()
 
 
 def main_kernel(
-    table_hbm, gate_hbm, up_hbm, grad_hbm, wd_hbm, wg_hbm, wu_hbm,
+    part_ref, table_hbm, gate_hbm, up_hbm, grad_hbm, wd_hbm, wg_hbm, wu_hbm,
     their_far, their_near, our_far, our_near,
     table, gate_v, up_v, grad, wd, w, small_sem, grad_sem, wd_sem, wg_sem, wu_sem,
 ):
-    _, d = grad.shape
+    d = w.shape[1]
     ff = wd.shape[0]
     blk = our_far.shape[0]
     step = d // CHUNKS
@@ -133,13 +169,7 @@
             ((gate_hbm, gate_v), (up_hbm, up_v), (table_hbm, table))
         )
     ]
-    loads = [
-        (
-            pltpu.make_async_copy(grad_hbm.at[:, c], grad.at[:, c], grad_sem.at[i]),
-            pltpu.make_async_copy(wd_hbm.at[:, c], wd.at[:, c], wd_sem.at[i]),
-        )
-        for i, c in enumerate(chunks)
-    ]
+    loads = load_chunks(grad_hbm, wd_hbm, grad, wd, grad_sem, wd_sem, HEAD)
     weights = [
         (
             pltpu.make_async_copy(wg_hbm.at[:, c], w.at[:ff, c], wg_sem.at[i]),
@@ -149,7 +179,7 @@
     ]
     for copy in small:
         copy.start()
-    for pair in loads + weights:
+    for pair in loads:
         for copy in pair:
             copy.start()
 
@@ -162,11 +192,8 @@
     slope = up * sig * (1.0 + gate * (1.0 - sig))
     per = blk // NZ
     pick = one_hot(rows_of(table[...], 3, NC * per, per))
-    hidden_grad = jnp.zeros(gate.shape, f32)
-    for pair, c in zip(loads, chunks):
-        for copy in pair:
-            copy.wait()
-        hidden_grad = hidden_grad + dot(wd[:, c], grad[:, c], ((1,), (1,)))
+    behind = [copy for pair in weights for copy in pair]
+    hidden_grad = part_ref[...] + contract(loads, grad, wd, behind)
     both = jnp.concatenate(
         [(hidden_grad * slope).astype(bf16), (hidden_grad * silu).astype(bf16)], axis=0
     )
@@ -313,43 +340,50 @@
         pltpu.VMEM((ff, tokens), bf16),
         pltpu.VMEM((ff, tokens), bf16),
     ]
-    (packed,) = call(
+    head = d // CHUNKS * HEAD
+    packed, part = call(
         pack_kernel,
-        [HBM] * 4,
-        [(NY, packed_rows, width)],
-        2 * tokens * tokens * ff,
-        4_000_000,
+        [HBM] * 5,
+        [(NY, packed_rows, width), (ff, tokens)],
+        tokens * ff * d,
+        7_000_000,
         small
         + [
             pltpu.VMEM((2, share, d), bf16),
             pltpu.VMEM((NY, 2 * PIECES * share, width), bf16),
             pltpu.VMEM((packed_rows - 2 * PIECES * share, width), bf16),
+            pltpu.VMEM((tokens, head), bf16),
+            pltpu.VMEM((ff, head), bf16),
             dma((3,)),
             dma((2,)),
             dma((NY,)),
             dma((NY,)),
+            dma((HEAD,)),
+            dma((HEAD,)),
         ],
         in_hbm=(0,),
         mib=63,
-    )(table, gate_t, up_t, grad_out)
+        dtype=(bf16, f32),
+    )(table, gate_t, up_t, grad_out, w_down)
     packed = lax.all_to_all(packed, "y", 0, 0)
 
     their_far, their_near, our_far, our_near = call(
         main_kernel,
-        [HBM] * 7,
+        [VMEM] + [HBM] * 7,
         [(blk, d), (3 * blk, d), (blk, d), (3 * blk, d)],
-        6 * tokens * ff * d,
-        15_000_000,
+        5 * tokens * ff * d,
+        12_000_000,
         small
         + [
-            pltpu.VMEM((tokens, d), bf16),
-            pltpu.VMEM((ff, d), bf16),
+            pltpu.VMEM((tokens, d - head), bf16),
+            pltpu.VMEM((ff, d - head), bf16),
             pltpu.VMEM((2 * ff, d), bf16),
             dma((3,)),
         ]
-        + [dma((CHUNKS,))] * 4,
+        + [dma((CHUNKS - HEAD,))] * 2
+        + [dma((CHUNKS,))] * 2,
         mib=58,
-    )(table, gate_t, up_t, grad_out, w_down, w_gate, w_up)
+    )(part, table, gate_t, up_t, grad_out, w_down, w_gate, w_up)
     their_far = lax.ppermute(their_far, "c", shift(NC, 1))
     their_near = lax.ppermute(their_near, "c", shift(NC, 1))
     (far,) = call(add_kernel, [VMEM] * 2, [(blk, d)], blk * d, 6 * blk * d)(

time: 110 us -> 112 us (1.018)
  waiting for transfers between devices: 44.3 us -> 46.9 us
    all_to_all x1, waiting for transfers between devices: 14.7 us -> 18.3 us  [local(): packed = lax.all_to_all(packed, 'y', 0, 0)]
  transfers between devices with their start and end apart: 10 -> 10, of which waited for: 5 -> 5; matrix products, arithmetic and copies ran while one was open for 1% -> 1% of each run, Pallas kernels for 14% -> 12%
where the time goes in v1:
time: 112 us; the launch traced here: 111 us
  waiting for transfers between devices  46.9 us (42%)
  starting transfers between devices  43.7 us (39%)
  Pallas kernels  18.8 us (17%)
    pallas_call x9, Pallas kernels, on_chip(): run(*(pltpu.with_memory_space_constraint(a, pltpu.VMEM) if s is VMEM else...  18.8 us
    all_to_all x1, waiting for transfers between devices, local(): packed = lax.all_to_all(packed, 'y', 0, 0)  18.3 us
    all_to_all x1, waiting for transfers between devices, local(): parts = lax.all_to_all(own, 'z', 0, 0)  15.4 us
    all_to_all x1, starting transfers between devices, local(): parts = lax.all_to_all(own, 'z', 0, 0)  14.2 us
    ppermute x1, waiting for transfers between devices, local(): via = lax.ppermute(via, ('x', 'c'), round_x(1))  7.71 us
    all_to_all x1, starting transfers between devices, local(): packed = lax.all_to_all(packed, 'y', 0, 0)  6.83 us
    ppermute x1, starting transfers between devices, local(): far = lax.ppermute(far, ('x', 'c'), round_x(1))  4.39 us
    ppermute x1, waiting for transfers between devices, local(): other = lax.ppermute(other, ('x', 'c'), round_x(-1))  3.82 us
  transfers between devices with their start and end apart: 10, of which 5 were waited for; matrix products, arithmetic and copies ran while one was open for 1% of the time, Pallas kernels for 12%

profile of v1, /device:TPU:65, one launch (start us, length us, event | category | flops | bytes accessed | tf_op | source)
XLA Modules:
  0.0 111.2 jit_solution(7137648001985477594)
XLA Ops:
  0.6 3.2 %shard_map.86 = (bf16[8,336,256]{2,1,0:T(8,128)(2,1)}, f32[176,192]{1,0:T(8,128)S(1)}) custom-call(s32[192,4]{1,0:T(8,128)} %constant.2.clone.table_hbm, bf16[176,192]{1,0:T(8,128)(2,1)} %bitcast.2, bf16[176,192]{1,0:T(8,128)(2,1)} %bitcast.4, bf16[192,8192]{1,0:T(8,128)(2,1)} %grad_hbm.3, bf16[176,8192]{1,0:T(8,128)(2,1)} %wd_hbm.3), custom_call_target="tpu_custom_call" | custom-call | flops 276824064 | bytes 7000000 | tf_op jit(solution)/shard_map/pallas_call | solution.py:312
  3.9 6.8 %all-to-all-start.1 = ((bf16[8,336,256]{2,1,0:T(8,128)(2,1)}), bf16[8,336,256]{2,1,0:T(8,128)(2,1)S(1)}, u32[]{:S(2)}, u32[]{:S(2)}) async-start(bf16[8,336,256]{2,1,0:T(8,128)(2,1)} %get-tuple-element.19), calls=%async_computation.1 | async-start | bytes 2752512 | tf_op jit(solution)/shard_map/all_to_all | solution.py:368
  10.7 6.9 %shard_map.87 = (bf16[24,8192]{1,0:T(8,128)(2,1)S(1)}, bf16[72,8192]{1,0:T(8,128)(2,1)}, bf16[24,8192]{1,0:T(8,128)(2,1)S(1)}, bf16[72,8192]{1,0:T(8,128)(2,1)S(1)}) custom-call(f32[176,192]{1,0:T(8,128)S(1)} %get-tuple-element.11.part_ref, s32[192,4]{1,0:T(8,128)} %constant.2.clone.table_hbm, bf16[176,192]{1,0:T(8,128)(2,1)} %bitcast.3, ...), custom_call_target="tpu_custom_call" | custom-call | flops 1384120320 | bytes 12000000 | tf_op jit(solution)/shard_map/pallas_call | solution.py:312
  17.7 2.9 %collective-permute-start = (bf16[72,8192]{1,0:T(8,128)(2,1)}, bf16[72,8192]{1,0:T(8,128)(2,1)}, u32[]{:S(2)}, u32[]{:S(2)}) collective-permute-start(bf16[72,8192]{1,0:T(8,128)(2,1)} %get-tuple-element.13), channel_id=1, source_target_pairs={{0,1},{1,0},{2,3},{3,2},{4,5},{5,4},{6,7},{7,6},{8,9},{9,8},{10,11... | collective-permute-start | bytes 3538952 | tf_op jit(solution)/shard_map/ppermute | solution.py:388
  20.5 1.9 %collective-permute-start.1 = (bf16[24,8192]{1,0:T(8,128)(2,1)S(1)}, bf16[24,8192]{1,0:T(8,128)(2,1)S(1)}, u32[]{:S(2)}, u32[]{:S(2)}) collective-permute-start(bf16[24,8192]{1,0:T(8,128)(2,1)S(1)} %get-tuple-element.17), channel_id=1, source_target_pairs={{0,1},{1,0},{2,3},{3,2},{4,5},{5,4},{6,7},{7,6},{8,9},{9,8},{10,11... | collective-permute-start | bytes 1179656 | tf_op jit(solution)/shard_map/ppermute | solution.py:387
  22.5 1.7 %collective-permute-done.1.b_ref = bf16[24,8192]{1,0:T(8,128)(2,1)S(1)} collective-permute-done((bf16[24,8192]{1,0:T(8,128)(2,1)S(1)}, bf16[24,8192]{1,0:T(8,128)(2,1)S(1)}, u32[]{:S(2)}, u32[]{:S(2)}) %collective-permute-start.1) | collective-permute-done | bytes 393248 | tf_op jit(solution)/shard_map/ppermute | solution.py:387
  24.2 0.1 shard_map.89
  24.2 4.4 %collective-permute-start.2 = (bf16[24,8192]{1,0:T(8,128)(2,1)S(1)}, bf16[24,8192]{1,0:T(8,128)(2,1)}, u32[]{:S(2)}, u32[]{:S(2)}) collective-permute-start(bf16[24,8192]{1,0:T(8,128)(2,1)S(1)} %shard_map.89), channel_id=1, source_target_pairs={{0,2},{1,7},{2,4},{3,1},{4,6},{5,3},{6,0},{7,5},{8,10},{9,15},{10,... | collective-permute-start | bytes 1179656 | tf_op jit(solution)/shard_map/ppermute | solution.py:392
  28.6 18.3 %all-to-all-done.1.own_ref = bf16[8,336,256]{2,1,0:T(8,128)(2,1)S(1)} async-done(((bf16[8,336,256]{2,1,0:T(8,128)(2,1)}), bf16[8,336,256]{2,1,0:T(8,128)(2,1)S(1)}, u32[]{:S(2)}, u32[]{:S(2)}) %all-to-all-start.1) | async-done | bytes 1376288 | tf_op jit(solution)/shard_map/all_to_all | solution.py:368
  46.9 1.0 slice.4
  47.9 3.1 %collective-permute-start.5 = (bf16[8,192,256]{2,1,0:T(8,128)(2,1)}, bf16[8,192,256]{2,1,0:T(8,128)(2,1)}, u32[]{:S(2)}, u32[]{:S(2)}) collective-permute-start(bf16[8,192,256]{2,1,0:T(8,128)(2,1)} %slice.4), channel_id=1, source_target_pairs={{0,6},{1,3},{2,0},{3,5},{4,2},{5,7},{6,4},{7,1},{8,14},{9,11},{10,... | collective-permute-start | bytes 2359304 | tf_op jit(solution)/shard_map/ppermute | solution.py:413
  51.0 0.0 collective-permute-done.b_ref
  51.0 1.5 %shard_map.88 = (f32[24,8192]{1,0:T(8,128)S(1)}, f32[24,8192]{1,0:T(8,128)S(1)}, bf16[24,8192]{1,0:T(8,128)(2,1)S(1)}) custom-call(bf16[72,8192]{1,0:T(8,128)(2,1)S(1)} %get-tuple-element.12.a_ref, bf16[72,8192]{1,0:T(8,128)(2,1)} %collective-permute-done.b_ref), custom_call_target="tpu_custom_call" | custom-call | flops 589824 | bytes 4325376 | tf_op jit(solution)/shard_map/pallas_call | solution.py:312
  52.5 0.0 collective-permute-done.2.b_ref
  52.6 1.1 shard_map.90
  53.6 3.4 %collective-permute-start.3 = (bf16[24,8192]{1,0:T(8,128)(2,1)S(1)}, bf16[24,8192]{1,0:T(8,128)(2,1)S(1)}, u32[]{:S(2)}, u32[]{:S(2)}) collective-permute-start(bf16[24,8192]{1,0:T(8,128)(2,1)S(1)} %shard_map.90), channel_id=1, source_target_pairs={{0,2},{1,7},{2,4},{3,1},{4,6},{5,3},{6,0},{7,5},{8,10},{9,15},{10,... | collective-permute-start | bytes 1179656 | tf_op jit(solution)/shard_map/ppermute | solution.py:403
  57.0 1.9 %collective-permute-start.4 = (bf16[24,8192]{1,0:T(8,128)(2,1)S(1)}, bf16[24,8192]{1,0:T(8,128)(2,1)S(1)}, u32[]{:S(2)}, u32[]{:S(2)}) collective-permute-start(bf16[24,8192]{1,0:T(8,128)(2,1)S(1)} %get-tuple-element.18), channel_id=1, source_target_pairs={{0,6},{1,3},{2,0},{3,5},{4,2},{5,7},{6,4},{7,1},{8,14},{9,11},{10,... | collective-permute-start | bytes 1179656 | tf_op jit(solution)/shard_map/ppermute | solution.py:401
  58.9 7.7 %collective-permute-done.3.via_ref = bf16[24,8192]{1,0:T(8,128)(2,1)S(1)} collective-permute-done((bf16[24,8192]{1,0:T(8,128)(2,1)S(1)}, bf16[24,8192]{1,0:T(8,128)(2,1)S(1)}, u32[]{:S(2)}, u32[]{:S(2)}) %collective-permute-start.3) | collective-permute-done | bytes 393248 | tf_op jit(solution)/shard_map/ppermute | solution.py:403
  66.6 3.8 %collective-permute-done.4.other_ref = bf16[24,8192]{1,0:T(8,128)(2,1)S(1)} collective-permute-done((bf16[24,8192]{1,0:T(8,128)(2,1)S(1)}, bf16[24,8192]{1,0:T(8,128)(2,1)S(1)}, u32[]{:S(2)}, u32[]{:S(2)}) %collective-permute-start.4) | collective-permute-done | bytes 393248 | tf_op jit(solution)/shard_map/ppermute | solution.py:401
  70.5 0.9 shard_map.91
  71.4 14.2 %all-to-all-start = ((bf16[12,2,8192]{2,1,0:T(2,128)(2,1)}), bf16[12,2,8192]{2,1,0:T(2,128)(2,1)S(1)}, u32[]{:S(2)}, u32[]{:S(2)}) async-start(bf16[12,2,8192]{2,1,0:T(2,128)(2,1)} %shard_map.91), calls=%async_computation | async-start | bytes 786432 | tf_op jit(solution)/shard_map/all_to_all | solution.py:407
  85.6 3.2 %collective-permute-start.7 = (bf16[8,192,256]{2,1,0:T(8,128)(2,1)}, bf16[8,192,256]{2,1,0:T(8,128)(2,1)S(1)}, u32[]{:S(2)}, u32[]{:S(2)}) collective-permute-start(bf16[8,192,256]{2,1,0:T(8,128)(2,1)} %slice.4), channel_id=1, source_target_pairs={{0,1},{1,0},{2,3},{3,2},{4,5},{5,4},{6,7},{7,6},{8,9},{9,8},{10,11... | collective-permute-start | bytes 2359304 | tf_op jit(solution)/shard_map/ppermute | solution.py:414
  88.8 0.0 collective-permute-done.5.side_ref
  88.8 1.9 %collective-permute-start.6 = (bf16[8,192,256]{2,1,0:T(8,128)(2,1)}, bf16[8,192,256]{2,1,0:T(8,128)(2,1)}, u32[]{:S(2)}, u32[]{:S(2)}) collective-permute-start(bf16[8,192,256]{2,1,0:T(8,128)(2,1)} %collective-permute-done.5.side_ref), channel_id=1, source_target_pairs={{0,1},{1,0},{2,3},{3,2},{4,5},{5,4},{6,7},{7,6},{8,9},{9,8},{10,11... | collective-permute-start | bytes 2359304 | tf_op jit(solution)/shard_map/ppermute | solution.py:415
  90.7 15.4 %all-to-all-done.parts_ref = bf16[12,2,8192]{2,1,0:T(2,128)(2,1)S(1)} async-done(((bf16[12,2,8192]{2,1,0:T(2,128)(2,1)}), bf16[12,2,8192]{2,1,0:T(2,128)(2,1)S(1)}, u32[]{:S(2)}, u32[]{:S(2)}) %all-to-all-start) | async-done | bytes 393248 | tf_op jit(solution)/shard_map/all_to_all | solution.py:407
  106.1 0.7 shard_map.92
  106.8 0.0 collective-permute-done.7.core_ref
  106.8 2.0 %shard_map.93.sum_ref = f32[176,1024]{1,0:T(8,128)S(1)} custom-call(bf16[8,336,256]{2,1,0:T(8,128)(2,1)S(1)} %all-to-all-done.1.own_ref, bf16[8,192,256]{2,1,0:T(8,128)(2,1)} %collective-permute-done.5.side_ref, bf16[8,192,256]{2,1,0:T(8,128)(2,1)S(1)} %collective-permute-done.7.core_ref), custom_call_target="tpu_custom_call" | custom-call | flops 415236096 | bytes 6000000 | tf_op jit(solution)/shard_map/pallas_call | solution.py:312
  108.9 0.0 collective-permute-done.6.side_ref
  108.9 2.3 %shard_map.94 = bf16[176,1024]{1,0:T(8,128)(2,1)} custom-call(bf16[8,336,256]{2,1,0:T(8,128)(2,1)S(1)} %all-to-all-done.1.own_ref, bf16[8,192,256]{2,1,0:T(8,128)(2,1)} %collective-permute-done.6.side_ref, f32[176,1024]{1,0:T(8,128)S(1)} %shard_map.93.sum_ref), custom_call_target="tpu_custom_call" | custom-call | flops 138412032 | bytes 3000000 | tf_op jit(solution)/shard_map/pallas_call | solution.py:312
Async XLA Ops:
  3.9 43.0 %all-to-all-start.1 = ((bf16[8,336,256]{2,1,0:T(8,128)(2,1)}), bf16[8,336,256]{2,1,0:T(8,128)(2,1)S(1)}, u32[]{:S(2)}, u32[]{:S(2)}) async-start(bf16[8,336,256]{2,1,0:T(8,128)(2,1)} %get-tuple-element.19), calls=%async_computation.1 | async-start | bytes 2752512 | tf_op jit(solution)/shard_map/all_to_all | solution.py:368
  17.7 33.4 %collective-permute-start = (bf16[72,8192]{1,0:T(8,128)(2,1)}, bf16[72,8192]{1,0:T(8,128)(2,1)}, u32[]{:S(2)}, u32[]{:S(2)}) collective-permute-start(bf16[72,8192]{1,0:T(8,128)(2,1)} %get-tuple-element.13), channel_id=1, source_target_pairs={{0,1},{1,0},{2,3},{3,2},{4,5},{5,4},{6,7},{7,6},{8,9},{9,8},{10,11... | collective-permute-start | bytes 3538952 | tf_op jit(solution)/shard_map/ppermute | solution.py:388
  20.5 3.6 %collective-permute-start.1 = (bf16[24,8192]{1,0:T(8,128)(2,1)S(1)}, bf16[24,8192]{1,0:T(8,128)(2,1)S(1)}, u32[]{:S(2)}, u32[]{:S(2)}) collective-permute-start(bf16[24,8192]{1,0:T(8,128)(2,1)S(1)} %get-tuple-element.17), channel_id=1, source_target_pairs={{0,1},{1,0},{2,3},{3,2},{4,5},{5,4},{6,7},{7,6},{8,9},{9,8},{10,11... | collective-permute-start | bytes 1179656 | tf_op jit(solution)/shard_map/ppermute | solution.py:387
  24.2 28.3 %collective-permute-start.2 = (bf16[24,8192]{1,0:T(8,128)(2,1)S(1)}, bf16[24,8192]{1,0:T(8,128)(2,1)}, u32[]{:S(2)}, u32[]{:S(2)}) collective-permute-start(bf16[24,8192]{1,0:T(8,128)(2,1)S(1)} %shard_map.89), channel_id=1, source_target_pairs={{0,2},{1,7},{2,4},{3,1},{4,6},{5,3},{6,0},{7,5},{8,10},{9,15},{10,... | collective-permute-start | bytes 1179656 | tf_op jit(solution)/shard_map/ppermute | solution.py:392
  47.9 40.9 %collective-permute-start.5 = (bf16[8,192,256]{2,1,0:T(8,128)(2,1)}, bf16[8,192,256]{2,1,0:T(8,128)(2,1)}, u32[]{:S(2)}, u32[]{:S(2)}) collective-permute-start(bf16[8,192,256]{2,1,0:T(8,128)(2,1)} %slice.4), channel_id=1, source_target_pairs={{0,6},{1,3},{2,0},{3,5},{4,2},{5,7},{6,4},{7,1},{8,14},{9,11},{10,... | collective-permute-start | bytes 2359304 | tf_op jit(solution)/shard_map/ppermute | solution.py:413
  53.6 13.0 %collective-permute-start.3 = (bf16[24,8192]{1,0:T(8,128)(2,1)S(1)}, bf16[24,8192]{1,0:T(8,128)(2,1)S(1)}, u32[]{:S(2)}, u32[]{:S(2)}) collective-permute-start(bf16[24,8192]{1,0:T(8,128)(2,1)S(1)} %shard_map.90), channel_id=1, source_target_pairs={{0,2},{1,7},{2,4},{3,1},{4,6},{5,3},{6,0},{7,5},{8,10},{9,15},{10,... | collective-permute-start | bytes 1179656 | tf_op jit(solution)/shard_map/ppermute | solution.py:403
  57.0 13.5 %collective-permute-start.4 = (bf16[24,8192]{1,0:T(8,128)(2,1)S(1)}, bf16[24,8192]{1,0:T(8,128)(2,1)S(1)}, u32[]{:S(2)}, u32[]{:S(2)}) collective-permute-start(bf16[24,8192]{1,0:T(8,128)(2,1)S(1)} %get-tuple-element.18), channel_id=1, source_target_pairs={{0,6},{1,3},{2,0},{3,5},{4,2},{5,7},{6,4},{7,1},{8,14},{9,11},{10,... | collective-permute-start | bytes 1179656 | tf_op jit(solution)/shard_map/ppermute | solution.py:401
  71.4 34.7 %all-to-all-start = ((bf16[12,2,8192]{2,1,0:T(2,128)(2,1)}), bf16[12,2,8192]{2,1,0:T(2,128)(2,1)S(1)}, u32[]{:S(2)}, u32[]{:S(2)}) async-start(bf16[12,2,8192]{2,1,0:T(2,128)(2,1)} %shard_map.91), calls=%async_computation | async-start | bytes 786432 | tf_op jit(solution)/shard_map/all_to_all | solution.py:407
  85.6 21.2 %collective-permute-start.7 = (bf16[8,192,256]{2,1,0:T(8,128)(2,1)}, bf16[8,192,256]{2,1,0:T(8,128)(2,1)S(1)}, u32[]{:S(2)}, u32[]{:S(2)}) collective-permute-start(bf16[8,192,256]{2,1,0:T(8,128)(2,1)} %slice.4), channel_id=1, source_target_pairs={{0,1},{1,0},{2,3},{3,2},{4,5},{5,4},{6,7},{7,6},{8,9},{9,8},{10,11... | collective-permute-start | bytes 2359304 | tf_op jit(solution)/shard_map/ppermute | solution.py:414
  88.8 20.1 %collective-permute-start.6 = (bf16[8,192,256]{2,1,0:T(8,128)(2,1)}, bf16[8,192,256]{2,1,0:T(8,128)(2,1)}, u32[]{:S(2)}, u32[]{:S(2)}) collective-permute-start(bf16[8,192,256]{2,1,0:T(8,128)(2,1)} %collective-permute-done.5.side_ref), channel_id=1, source_target_pairs={{0,1},{1,0},{2,3},{3,2},{4,5},{5,4},{6,7},{7,6},{8,9},{9,8},{10,11... | collective-permute-start | bytes 2359304 | tf_op jit(solution)/shard_map/ppermute | solution.py:415

commit v2 on v1

--- a/solution.py
+++ b/solution.py
@@ -263,13 +263,19 @@
             g[rows, b * width : (b + 1) * width] = piece.reshape(block, width)
 
 
-def down_kernel(own_ref, side_ref, core_ref, out_ref, h, g):
+def down_kernel(own_ref, side_ref, side2_ref, core_ref, next_ref, out_ref, h, g):
     def piece_of(jk, b, share):
-        first = (jk % NX // 2 * PIECES + b) * share
-        ref = side_ref if jk % 2 else (own_ref if jk < NX else core_ref)
+        first = b * share
+        if jk % 2 == 0:
+            first = (jk % NX // 2 * PIECES + b) * share
+            ref = own_ref if jk < NX else core_ref
+        elif jk < NX:
+            ref = side_ref if jk == 1 else side2_ref
+        else:
+            ref = next_ref
         return ref[:, first : first + share, :]
 
-    gather_rows((0, 1, 2, 3, NX, NX + 2), piece_of, own_ref, h, g)
+    gather_rows((0, 1, 2, 3, NX, NX + 1, NX + 2), piece_of, own_ref, h, g)
     left = h[...]
     width = own_ref.shape[2]
     for b in range(PIECES):
@@ -279,10 +285,9 @@
 
 def last_kernel(own_ref, side_ref, sum_ref, out_ref, h, g):
     def piece_of(jk, b, share):
-        first = (jk % NX // 2 * PIECES + b) * share
-        return side_ref[:, first : first + share, :]
-
-    gather_rows((NX + 1, NX + 3), piece_of, own_ref, h, g)
+        return side_ref[:, b * share : (b + 1) * share, :]
+
+    gather_rows((NX + 3,), piece_of, own_ref, h, g)
     left = h[...]
     width = own_ref.shape[2]
     for b in range(PIECES):
@@ -410,19 +415,22 @@
     )(parts)
 
     mine = packed[:, : 2 * PIECES * share, :]
-    side = lax.ppermute(mine, ("x", "c"), round_x(-1))
+    part_rows = PIECES * share
+    side = lax.ppermute(mine[:, :part_rows], ("x", "c"), round_x(-1))
+    side2 = lax.ppermute(mine[:, part_rows:], ("x", "c"), round_x(-1))
     core = lax.ppermute(mine, "c", shift(NC, 1))
     side_core = lax.ppermute(side, "c", shift(NC, 1))
-    early, late = 6 * NY * share, 2 * NY * share
+    side_core2 = lax.ppermute(side2, "c", shift(NC, 1))
+    early, late = 7 * NY * share, NY * share
     (part,) = call(
         down_kernel,
-        [VMEM] * 3,
+        [VMEM] * 5,
         [(ff, cols)],
         2 * early * ff * cols,
         6_000_000,
         [pltpu.VMEM((early, ff), bf16), pltpu.VMEM((early, cols), bf16)],
         dtype=(f32,),
-    )(packed, side, core)
+    )(packed, side, side2, core, side_core)
     (down_grad,) = call(
         last_kernel,
         [VMEM] * 3,
@@ -431,7 +439,7 @@
         3_000_000,
         [pltpu.VMEM((late, ff), bf16), pltpu.VMEM((late, cols), bf16)],
         auto=True,
-    )(packed, side_core, part)
+    )(packed, side_core2, part)
     return (input_grad, down_grad)
 
 

time: 112 us -> 89 us (0.79)
  the two profiles are of different devices: /device:TPU:65 before, /device:TPU:1 now
where the time goes in v2:
time: 89 us; the launch traced here: 88.4 us
  starting transfers between devices  46.7 us (52%)
  waiting for transfers between devices  25.5 us (29%)
  Pallas kernels  14.5 us (16%)
  local copies, waits for them, and re-layouts  1.02 us (1%)
    pallas_call x9, Pallas kernels, on_chip(): run(*(pltpu.with_memory_space_constraint(a, pltpu.VMEM) if s is VMEM else...  14.5 us
    all_to_all x1, starting transfers between devices, local(): parts = lax.all_to_all(own, 'z', 0, 0)  9.41 us
    ppermute x1, starting transfers between devices, local(): their_near = lax.ppermute(their_near, 'c', shift(NC, 1))  8.33 us
    ppermute x1, waiting for transfers between devices, local(): other = lax.ppermute(other, ('x', 'c'), round_x(-1))  7.79 us
    all_to_all x1, starting transfers between devices, local(): packed = lax.all_to_all(packed, 'y', 0, 0)  7.65 us
    ppermute x1, waiting for transfers between devices, local(): far = lax.ppermute(far, ('x', 'c'), round_x(1))  6.62 us
    ppermute x1, waiting for transfers between devices, local(): side2 = lax.ppermute(mine[:, part_rows:], ('x', 'c'), round_x(-1))  4.99 us
    ppermute x1, starting transfers between devices, local(): core = lax.ppermute(mine, 'c', shift(NC, 1))  4.16 us
  transfers between devices with their start and end apart: 12, of which 6 were waited for; matrix products, arithmetic and copies ran while one was open for 1% of the time, Pallas kernels for 11%

profile of v2, /device:TPU:1, one launch (start us, length us, event | category | flops | bytes accessed | tf_op | source)
XLA Modules:
  0.0 88.4 jit_solution(2219722279202055030)
XLA Ops:
  0.6 3.3 %shard_map.86 = (bf16[8,336,256]{2,1,0:T(8,128)(2,1)}, f32[176,192]{1,0:T(8,128)S(1)}) custom-call(s32[192,4]{1,0:T(8,128)} %constant.2.clone.table_hbm, bf16[176,192]{1,0:T(8,128)(2,1)} %bitcast.2, bf16[176,192]{1,0:T(8,128)(2,1)} %bitcast.4, bf16[192,8192]{1,0:T(8,128)(2,1)} %grad_hbm.3, bf16[176,8192]{1,0:T(8,128)(2,1)} %wd_hbm.3), custom_call_target="tpu_custom_call" | custom-call | flops 276824064 | bytes 7000000 | tf_op jit(solution)/shard_map/pallas_call | solution.py:317
  3.9 7.7 %all-to-all-start.1 = ((bf16[8,336,256]{2,1,0:T(8,128)(2,1)}), bf16[8,336,256]{2,1,0:T(8,128)(2,1)S(1)}, u32[]{:S(2)}, u32[]{:S(2)}) async-start(bf16[8,336,256]{2,1,0:T(8,128)(2,1)} %get-tuple-element.19), calls=%async_computation.1 | async-start | bytes 2752512 | tf_op jit(solution)/shard_map/all_to_all | solution.py:373
  11.5 5.9 %shard_map.87 = (bf16[24,8192]{1,0:T(8,128)(2,1)S(1)}, bf16[72,8192]{1,0:T(8,128)(2,1)S(1)}, bf16[24,8192]{1,0:T(8,128)(2,1)S(1)}, bf16[72,8192]{1,0:T(8,128)(2,1)S(1)}) custom-call(f32[176,192]{1,0:T(8,128)S(1)} %get-tuple-element.11.part_ref, s32[192,4]{1,0:T(8,128)} %constant.2.clone.table_hbm, bf16[176,192]{1,0:T(8,128)(2,1)} %bitcast.3, ...), custom_call_target="tpu_custom_call" | custom-call | flops 1384120320 | bytes 12000000 | tf_op jit(solution)/shard_map/pallas_call | solution.py:317
  17.5 8.3 %collective-permute-start = (bf16[72,8192]{1,0:T(8,128)(2,1)S(1)}, bf16[72,8192]{1,0:T(8,128)(2,1)S(1)}, u32[]{:S(2)}, u32[]{:S(2)}) collective-permute-start(bf16[72,8192]{1,0:T(8,128)(2,1)S(1)} %get-tuple-element.13), channel_id=1, source_target_pairs={{0,1},{1,0},{2,3},{3,2},{4,5},{5,4},{6,7},{7,6},{8,9},{9,8},{10,11... | collective-permute-start | bytes 3538952 | tf_op jit(solution)/shard_map/ppermute | solution.py:393
  25.8 1.9 %collective-permute-start.1 = (bf16[24,8192]{1,0:T(8,128)(2,1)S(1)}, bf16[24,8192]{1,0:T(8,128)(2,1)S(1)}, u32[]{:S(2)}, u32[]{:S(2)}) collective-permute-start(bf16[24,8192]{1,0:T(8,128)(2,1)S(1)} %get-tuple-element.17), channel_id=1, source_target_pairs={{0,1},{1,0},{2,3},{3,2},{4,5},{5,4},{6,7},{7,6},{8,9},{9,8},{10,11... | collective-permute-start | bytes 1179656 | tf_op jit(solution)/shard_map/ppermute | solution.py:392
  27.7 1.7 %collective-permute-done.1.b_ref = bf16[24,8192]{1,0:T(8,128)(2,1)S(1)} collective-permute-done((bf16[24,8192]{1,0:T(8,128)(2,1)S(1)}, bf16[24,8192]{1,0:T(8,128)(2,1)S(1)}, u32[]{:S(2)}, u32[]{:S(2)}) %collective-permute-start.1) | collective-permute-done | bytes 393248 | tf_op jit(solution)/shard_map/ppermute | solution.py:392
  29.4 0.1 shard_map.89
  29.5 1.9 %collective-permute-start.2 = (bf16[24,8192]{1,0:T(8,128)(2,1)S(1)}, bf16[24,8192]{1,0:T(8,128)(2,1)S(1)}, u32[]{:S(2)}, u32[]{:S(2)}) collective-permute-start(bf16[24,8192]{1,0:T(8,128)(2,1)S(1)} %shard_map.89), channel_id=1, source_target_pairs={{0,2},{1,7},{2,4},{3,1},{4,6},{5,3},{6,0},{7,5},{8,10},{9,15},{10,... | collective-permute-start | bytes 1179656 | tf_op jit(solution)/shard_map/ppermute | solution.py:397
  31.5 0.0 collective-permute-done.b_ref
  31.5 0.2 shard_map.88
  31.7 6.6 %collective-permute-done.2.b_ref = bf16[24,8192]{1,0:T(8,128)(2,1)S(1)} collective-permute-done((bf16[24,8192]{1,0:T(8,128)(2,1)S(1)}, bf16[24,8192]{1,0:T(8,128)(2,1)S(1)}, u32[]{:S(2)}, u32[]{:S(2)}) %collective-permute-start.2) | collective-permute-done | bytes 393248 | tf_op jit(solution)/shard_map/ppermute | solution.py:397
  38.3 0.1 shard_map.90
  38.4 3.1 %collective-permute-start.3 = (bf16[24,8192]{1,0:T(8,128)(2,1)S(1)}, bf16[24,8192]{1,0:T(8,128)(2,1)S(1)}, u32[]{:S(2)}, u32[]{:S(2)}) collective-permute-start(bf16[24,8192]{1,0:T(8,128)(2,1)S(1)} %shard_map.90), channel_id=1, source_target_pairs={{0,2},{1,7},{2,4},{3,1},{4,6},{5,3},{6,0},{7,5},{8,10},{9,15},{10,... | collective-permute-start | bytes 1179656 | tf_op jit(solution)/shard_map/ppermute | solution.py:408
  41.6 2.2 %collective-permute-start.4 = (bf16[24,8192]{1,0:T(8,128)(2,1)S(1)}, bf16[24,8192]{1,0:T(8,128)(2,1)S(1)}, u32[]{:S(2)}, u32[]{:S(2)}) collective-permute-start(bf16[24,8192]{1,0:T(8,128)(2,1)S(1)} %get-tuple-element.18), channel_id=1, source_target_pairs={{0,6},{1,3},{2,0},{3,5},{4,2},{5,7},{6,4},{7,1},{8,14},{9,11},{10,... | collective-permute-start | bytes 1179656 | tf_op jit(solution)/shard_map/ppermute | solution.py:406
  43.7 3.5 %collective-permute-done.3.via_ref = bf16[24,8192]{1,0:T(8,128)(2,1)S(1)} collective-permute-done((bf16[24,8192]{1,0:T(8,128)(2,1)S(1)}, bf16[24,8192]{1,0:T(8,128)(2,1)S(1)}, u32[]{:S(2)}, u32[]{:S(2)}) %collective-permute-start.3) | collective-permute-done | bytes 393248 | tf_op jit(solution)/shard_map/ppermute | solution.py:408
  47.2 7.8 %collective-permute-done.4.other_ref = bf16[24,8192]{1,0:T(8,128)(2,1)S(1)} collective-permute-done((bf16[24,8192]{1,0:T(8,128)(2,1)S(1)}, bf16[24,8192]{1,0:T(8,128)(2,1)S(1)}, u32[]{:S(2)}, u32[]{:S(2)}) %collective-permute-start.4) | collective-permute-done | bytes 393248 | tf_op jit(solution)/shard_map/ppermute | solution.py:406
  55.0 0.9 %shard_map.91 = bf16[12,2,8192]{2,1,0:T(2,128)(2,1)} custom-call(f32[24,8192]{1,0:T(8,128)S(1)} %get-tuple-element.14.own_ref, bf16[24,8192]{1,0:T(8,128)(2,1)S(1)} %collective-permute-done.3.via_ref, bf16[24,8192]{1,0:T(8,128)(2,1)S(1)} %collective-permute-done.4.other_ref), custom_call_target="tpu_custom_call" | custom-call | flops 393216 | bytes 1966080 | tf_op jit(solution)/shard_map/pallas_call | solution.py:317
  55.9 0.0 all-to-all-done.1.own_ref
  55.9 9.4 %all-to-all-start = ((bf16[12,2,8192]{2,1,0:T(2,128)(2,1)}), bf16[12,2,8192]{2,1,0:T(2,128)(2,1)S(1)}, u32[]{:S(2)}, u32[]{:S(2)}) async-start(bf16[12,2,8192]{2,1,0:T(2,128)(2,1)} %shard_map.91), calls=%async_computation | async-start | bytes 786432 | tf_op jit(solution)/shard_map/all_to_all | solution.py:412
  65.4 0.1 fusion
  65.4 1.9 %collective-permute-start.7 = (bf16[8,96,256]{2,1,0:T(8,128)(2,1)S(1)}, bf16[8,96,256]{2,1,0:T(8,128)(2,1)}, u32[]{:S(2)}, u32[]{:S(2)}) collective-permute-start(bf16[8,96,256]{2,1,0:T(8,128)(2,1)S(1)} %get-tuple-element.20), channel_id=1, source_target_pairs={{0,6},{1,3},{2,0},{3,5},{4,2},{5,7},{6,4},{7,1},{8,14},{9,11},{10,... | collective-permute-start | bytes 1179656 | tf_op jit(solution)/shard_map/ppermute | solution.py:419
  67.4 0.9 %slice.16 = bf16[8,192,256]{2,1,0:T(8,128)(2,1)} slice(bf16[8,336,256]{2,1,0:T(8,128)(2,1)S(1)} %all-to-all-done.1.own_ref), slice={[0:8], [0:192], [0:256]} | slice | bytes 1572864 | tf_op jit(solution)/shard_map/slice | solution.py:417
  68.3 4.2 %collective-permute-start.8 = (bf16[8,192,256]{2,1,0:T(8,128)(2,1)}, bf16[8,192,256]{2,1,0:T(8,128)(2,1)S(1)}, u32[]{:S(2)}, u32[]{:S(2)}) collective-permute-start(bf16[8,192,256]{2,1,0:T(8,128)(2,1)} %slice.16), channel_id=1, source_target_pairs={{0,1},{1,0},{2,3},{3,2},{4,5},{5,4},{6,7},{7,6},{8,9},{9,8},{10,11... | collective-permute-start | bytes 2359304 | tf_op jit(solution)/shard_map/ppermute | solution.py:421
  72.5 1.9 %collective-permute-start.5 = (bf16[8,96,256]{2,1,0:T(8,128)(2,1)S(1)}, bf16[8,96,256]{2,1,0:T(8,128)(2,1)}, u32[]{:S(2)}, u32[]{:S(2)}) collective-permute-start(bf16[8,96,256]{2,1,0:T(8,128)(2,1)S(1)} %get-tuple-element.21), channel_id=1, source_target_pairs={{0,6},{1,3},{2,0},{3,5},{4,2},{5,7},{6,4},{7,1},{8,14},{9,11},{10,... | collective-permute-start | bytes 1179656 | tf_op jit(solution)/shard_map/ppermute | solution.py:420
  74.4 0.9 collective-permute-done.7.side_ref
  75.3 2.2 %collective-permute-start.9 = (bf16[8,96,256]{2,1,0:T(8,128)(2,1)}, bf16[8,96,256]{2,1,0:T(8,128)(2,1)}, u32[]{:S(2)}, u32[]{:S(2)}) collective-permute-start(bf16[8,96,256]{2,1,0:T(8,128)(2,1)} %collective-permute-done.7.side_ref), channel_id=1, source_target_pairs={{0,1},{1,0},{2,3},{3,2},{4,5},{5,4},{6,7},{7,6},{8,9},{9,8},{10,11... | collective-permute-start | bytes 1179656 | tf_op jit(solution)/shard_map/ppermute | solution.py:422
  77.5 5.0 %collective-permute-done.5.side2_ref = bf16[8,96,256]{2,1,0:T(8,128)(2,1)} collective-permute-done((bf16[8,96,256]{2,1,0:T(8,128)(2,1)S(1)}, bf16[8,96,256]{2,1,0:T(8,128)(2,1)}, u32[]{:S(2)}, u32[]{:S(2)}) %collective-permute-start.5) | collective-permute-done | bytes 393248 | tf_op jit(solution)/shard_map/ppermute | solution.py:420
  82.5 1.9 %collective-permute-start.6 = (bf16[8,96,256]{2,1,0:T(8,128)(2,1)}, bf16[8,96,256]{2,1,0:T(8,128)(2,1)S(1)}, u32[]{:S(2)}, u32[]{:S(2)}) collective-permute-start(bf16[8,96,256]{2,1,0:T(8,128)(2,1)} %collective-permute-done.5.side2_ref), channel_id=1, source_target_pairs={{0,1},{1,0},{2,3},{3,2},{4,5},{5,4},{6,7},{7,6},{8,9},{9,8},{10,11... | collective-permute-start | bytes 1179656 | tf_op jit(solution)/shard_map/ppermute | solution.py:423
  84.4 0.0 all-to-all-done.parts_ref
  84.4 0.7 shard_map.92
  85.1 0.0 collective-permute-done.9.next_ref
  85.1 0.0 collective-permute-done.8.core_ref
  85.1 2.2 %shard_map.93.sum_ref = f32[176,1024]{1,0:T(8,128)S(1)} custom-call(bf16[8,336,256]{2,1,0:T(8,128)(2,1)S(1)} %all-to-all-done.1.own_ref, bf16[8,96,256]{2,1,0:T(8,128)(2,1)} %collective-permute-done.7.side_ref, bf16[8,96,256]{2,1,0:T(8,128)(2,1)} %collective-permute-done.5.side2_ref, bf16[8,192,256]{2,1,0:T(8,128)(2,1)S(1)} %collective-permute-done.8.core_ref, ...), custom_call_target="tpu_custom_call" | custom-call | flops 484442112 | bytes 6000000 | tf_op jit(solution)/shard_map/pallas_call | solution.py:317
  87.3 0.0 collective-permute-done.6.side_ref
  87.4 1.1 %shard_map.94 = bf16[176,1024]{1,0:T(8,128)(2,1)} custom-call(bf16[8,336,256]{2,1,0:T(8,128)(2,1)S(1)} %all-to-all-done.1.own_ref, bf16[8,96,256]{2,1,0:T(8,128)(2,1)S(1)} %collective-permute-done.6.side_ref, f32[176,1024]{1,0:T(8,128)S(1)} %shard_map.93.sum_ref), custom_call_target="tpu_custom_call" | custom-call | flops 69206016 | bytes 3000000 | tf_op jit(solution)/shard_map/pallas_call | solution.py:317
Async XLA Ops:
  3.9 52.1 %all-to-all-start.1 = ((bf16[8,336,256]{2,1,0:T(8,128)(2,1)}), bf16[8,336,256]{2,1,0:T(8,128)(2,1)S(1)}, u32[]{:S(2)}, u32[]{:S(2)}) async-start(bf16[8,336,256]{2,1,0:T(8,128)(2,1)} %get-tuple-element.19), calls=%async_computation.1 | async-start | bytes 2752512 | tf_op jit(solution)/shard_map/all_to_all | solution.py:373
  17.5 14.0 %collective-permute-start = (bf16[72,8192]{1,0:T(8,128)(2,1)S(1)}, bf16[72,8192]{1,0:T(8,128)(2,1)S(1)}, u32[]{:S(2)}, u32[]{:S(2)}) collective-permute-start(bf16[72,8192]{1,0:T(8,128)(2,1)S(1)} %get-tuple-element.13), channel_id=1, source_target_pairs={{0,1},{1,0},{2,3},{3,2},{4,5},{5,4},{6,7},{7,6},{8,9},{9,8},{10,11... | collective-permute-start | bytes 3538952 | tf_op jit(solution)/shard_map/ppermute | solution.py:393
  25.8 3.6 %collective-permute-start.1 = (bf16[24,8192]{1,0:T(8,128)(2,1)S(1)}, bf16[24,8192]{1,0:T(8,128)(2,1)S(1)}, u32[]{:S(2)}, u32[]{:S(2)}) collective-permute-start(bf16[24,8192]{1,0:T(8,128)(2,1)S(1)} %get-tuple-element.17), channel_id=1, source_target_pairs={{0,1},{1,0},{2,3},{3,2},{4,5},{5,4},{6,7},{7,6},{8,9},{9,8},{10,11... | collective-permute-start | bytes 1179656 | tf_op jit(solution)/shard_map/ppermute | solution.py:392
  29.5 8.8 %collective-permute-start.2 = (bf16[24,8192]{1,0:T(8,128)(2,1)S(1)}, bf16[24,8192]{1,0:T(8,128)(2,1)S(1)}, u32[]{:S(2)}, u32[]{:S(2)}) collective-permute-start(bf16[24,8192]{1,0:T(8,128)(2,1)S(1)} %shard_map.89), channel_id=1, source_target_pairs={{0,2},{1,7},{2,4},{3,1},{4,6},{5,3},{6,0},{7,5},{8,10},{9,15},{10,... | collective-permute-start | bytes 1179656 | tf_op jit(solution)/shard_map/ppermute | solution.py:397
  38.4 8.8 %collective-permute-start.3 = (bf16[24,8192]{1,0:T(8,128)(2,1)S(1)}, bf16[24,8192]{1,0:T(8,128)(2,1)S(1)}, u32[]{:S(2)}, u32[]{:S(2)}) collective-permute-start(bf16[24,8192]{1,0:T(8,128)(2,1)S(1)} %shard_map.90), channel_id=1, source_target_pairs={{0,2},{1,7},{2,4},{3,1},{4,6},{5,3},{6,0},{7,5},{8,10},{9,15},{10,... | collective-permute-start | bytes 1179656 | tf_op jit(solution)/shard_map/ppermute | solution.py:408
  41.6 13.5 %collective-permute-start.4 = (bf16[24,8192]{1,0:T(8,128)(2,1)S(1)}, bf16[24,8192]{1,0:T(8,128)(2,1)S(1)}, u32[]{:S(2)}, u32[]{:S(2)}) collective-permute-start(bf16[24,8192]{1,0:T(8,128)(2,1)S(1)} %get-tuple-element.18), channel_id=1, source_target_pairs={{0,6},{1,3},{2,0},{3,5},{4,2},{5,7},{6,4},{7,1},{8,14},{9,11},{10,... | collective-permute-start | bytes 1179656 | tf_op jit(solution)/shard_map/ppermute | solution.py:406
  55.9 28.5 %all-to-all-start = ((bf16[12,2,8192]{2,1,0:T(2,128)(2,1)}), bf16[12,2,8192]{2,1,0:T(2,128)(2,1)S(1)}, u32[]{:S(2)}, u32[]{:S(2)}) async-start(bf16[12,2,8192]{2,1,0:T(2,128)(2,1)} %shard_map.91), calls=%async_computation | async-start | bytes 786432 | tf_op jit(solution)/shard_map/all_to_all | solution.py:412
  65.4 9.8 %collective-permute-start.7 = (bf16[8,96,256]{2,1,0:T(8,128)(2,1)S(1)}, bf16[8,96,256]{2,1,0:T(8,128)(2,1)}, u32[]{:S(2)}, u32[]{:S(2)}) collective-permute-start(bf16[8,96,256]{2,1,0:T(8,128)(2,1)S(1)} %get-tuple-element.20), channel_id=1, source_target_pairs={{0,6},{1,3},{2,0},{3,5},{4,2},{5,7},{6,4},{7,1},{8,14},{9,11},{10,... | collective-permute-start | bytes 1179656 | tf_op jit(solution)/shard_map/ppermute | solution.py:419
  68.3 16.8 %collective-permute-start.8 = (bf16[8,192,256]{2,1,0:T(8,128)(2,1)}, bf16[8,192,256]{2,1,0:T(8,128)(2,1)S(1)}, u32[]{:S(2)}, u32[]{:S(2)}) collective-permute-start(bf16[8,192,256]{2,1,0:T(8,128)(2,1)} %slice.16), channel_id=1, source_target_pairs={{0,1},{1,0},{2,3},{3,2},{4,5},{5,4},{6,7},{7,6},{8,9},{9,8},{10,11... | collective-permute-start | bytes 2359304 | tf_op jit(solution)/shard_map/ppermute | solution.py:421
  72.5 10.0 %collective-permute-start.5 = (bf16[8,96,256]{2,1,0:T(8,128)(2,1)S(1)}, bf16[8,96,256]{2,1,0:T(8,128)(2,1)}, u32[]{:S(2)}, u32[]{:S(2)}) collective-permute-start(bf16[8,96,256]{2,1,0:T(8,128)(2,1)S(1)} %get-tuple-element.21), channel_id=1, source_target_pairs={{0,6},{1,3},{2,0},{3,5},{4,2},{5,7},{6,4},{7,1},{8,14},{9,11},{10,... | collective-permute-start | bytes 1179656 | tf_op jit(solution)/shard_map/ppermute | solution.py:420
  75.3 9.9 %collective-permute-start.9 = (bf16[8,96,256]{2,1,0:T(8,128)(2,1)}, bf16[8,96,256]{2,1,0:T(8,128)(2,1)}, u32[]{:S(2)}, u32[]{:S(2)}) collective-permute-start(bf16[8,96,256]{2,1,0:T(8,128)(2,1)} %collective-permute-done.7.side_ref), channel_id=1, source_target_pairs={{0,1},{1,0},{2,3},{3,2},{4,5},{5,4},{6,7},{7,6},{8,9},{9,8},{10,11... | collective-permute-start | bytes 1179656 | tf_op jit(solution)/shard_map/ppermute | solution.py:422
  82.5 4.8 %collective-permute-start.6 = (bf16[8,96,256]{2,1,0:T(8,128)(2,1)}, bf16[8,96,256]{2,1,0:T(8,128)(2,1)S(1)}, u32[]{:S(2)}, u32[]{:S(2)}) collective-permute-start(bf16[8,96,256]{2,1,0:T(8,128)(2,1)} %collective-permute-done.5.side2_ref), channel_id=1, source_target_pairs={{0,1},{1,0},{2,3},{3,2},{4,5},{5,4},{6,7},{7,6},{8,9},{9,8},{10,11... | collective-permute-start | bytes 1179656 | tf_op jit(solution)/shard_map/ppermute | solution.py:423
